TPU v7x, 32 devices: a whole 2x2x4 slice. The times are simulated.
32 devices in a mesh: fsdp: 8 (over z, y), tensor: 4 (over x, core).
Axes of the slice: x: 2, y: 2, z: 4, core: 2. Of those that a mesh axis runs over, the one named last changes fastest.
Arguments:
- block_input: bfloat16 [32768, 512], P(('fsdp', 'tensor')), may hold values from -6 to 6
- segments: int32 [32768], P('fsdp'), may hold values from 0 to 6, as said below
- ln_gain: bfloat16 [512], P('fsdp'), may hold values from 0.5 to 1.5
- ln_bias: bfloat16 [512], P('fsdp'), may hold values from -3 to 3
- b_real: bfloat16 [512, 256], P('fsdp', 'tensor'), may hold values from -0.1875 to 0.1875
- b_imag: bfloat16 [512, 256], P('fsdp', 'tensor'), may hold values from -0.1875 to 0.1875
- c_real: bfloat16 [512, 256], P('fsdp', 'tensor'), may hold values from -0.25 to 0.25
- c_imag: bfloat16 [512, 256], P('fsdp', 'tensor'), may hold values from -0.25 to 0.25
- nu_log: bfloat16 [256], P('fsdp'), may hold values from -9.1875 to -3
- theta_log: bfloat16 [256], P('fsdp'), may hold values from -4 to -1
- gamma_log: bfloat16 [256], P('fsdp'), may hold values from -0.5 to 0.5
- d_skip: bfloat16 [512], P('fsdp'), may hold values from -4 to 4
- w_value: bfloat16 [512, 512], P('fsdp', 'tensor'), may hold values from -0.25 to 0.25
- w_gate: bfloat16 [512, 512], P('fsdp', 'tensor'), may hold values from -0.25 to 0.25
- b_value: bfloat16 [512], P('fsdp'), may hold values from -3 to 3
- b_gate: bfloat16 [512], P('fsdp'), may hold values from -3 to 3
- out_grad: bfloat16 [32768, 512], P(('fsdp', 'tensor')), may hold values from -6 to 6
Outputs:
- mixed: bfloat16 [32768, 512], P(('fsdp', 'tensor'))
- input_grad: float32 [32768, 512], P(('fsdp', 'tensor'))
- ln_gain_grad: float32 [512], P('fsdp')
- ln_bias_grad: float32 [512], P('fsdp')
- b_real_grad: float32 [512, 256], P('fsdp', 'tensor')
- b_imag_grad: float32 [512, 256], P('fsdp', 'tensor')
- c_real_grad: float32 [512, 256], P('fsdp', 'tensor')
- c_imag_grad: float32 [512, 256], P('fsdp', 'tensor')
- nu_grad: float32 [256], P('fsdp')
- theta_grad: float32 [256], P('fsdp')
- gamma_grad: float32 [256], P('fsdp')
- skip_grad: float32 [512], P('fsdp')
- value_weight_grad: float32 [512, 512], P('fsdp', 'tensor')
- gate_weight_grad: float32 [512, 512], P('fsdp', 'tensor')
- value_bias_grad: float32 [512], P('fsdp')
- gate_bias_grad: float32 [512], P('fsdp')
Inputs may be any that keep to these rules, and one draw needn't show every extreme that they name: `segments`: in each sequence of 2048 tokens the document numbers start at 1, rise by one at each of 5 boundaries that lie in the first three quarters, and all of 1 to 6 occur; the last 1 to 512 tokens are padding with number 0.
All inputs are finite; a program needn't handle non-finite values.
Results may differ from a plain program's by a relative error of at most 0.02.
Values may be sent and summed in bfloat16 or wider, within the bound.
No kernel may reach another device: no remote copies, remote signals or barrier semaphores. Data moves between devices by JAX's collectives and lax.ppermute only.
A program may use at most 128 MiB of HBM per device.

v0:
```python
import math
import jax
import jax.numpy as jnp
from jax import lax
from jax.sharding import PartitionSpec as P

SEQ_LEN = 2048
norm_epsilon = 1e-05


def complex_product(left, right):
    half_width = left.shape[-1] // 2
    left_re = left[..., :half_width]
    left_im = left[..., half_width:]
    right_re = right[..., :half_width]
    right_im = right[..., half_width:]
    return jnp.concatenate(
        [left_re * right_re - left_im * right_im, left_re * right_im + left_im * right_re], axis=-1
    )


def linear_chain(earlier, later):
    return (complex_product(later[0], earlier[0]), complex_product(later[0], earlier[1]) + later[1])


def blocked_chain(decay, source, reverse):
    rows, width = source.shape
    block = math.gcd(rows, 16)
    count = rows // block
    decay_blocks = decay.reshape(count, block, width)
    source_blocks = source.reshape(count, block, width)
    order = list(range(block - 1, -1, -1)) if reverse else list(range(block))
    decay_parts = [None] * block
    local_parts = [None] * block
    running_decay = None
    running_local = None
    for place in order:
        decay_here = decay_blocks[:, place]
        source_here = source_blocks[:, place]
        if running_decay is None:
            running_decay = decay_here
            running_local = source_here
        else:
            running_decay, running_local = linear_chain(
                (running_decay, running_local), (decay_here, source_here)
            )
        decay_parts[place] = running_decay
        local_parts[place] = running_local
    decay_cum = jnp.stack(decay_parts, axis=1)
    local = jnp.stack(local_parts, axis=1)
    edge = 0 if reverse else block - 1
    _, carried = lax.associative_scan(
        linear_chain, (decay_parts[edge], local_parts[edge]), reverse=reverse, axis=0
    )
    zero_row = jnp.zeros((1, width), jnp.float32)
    if reverse:
        incoming = jnp.concatenate([carried[1:], zero_row], axis=0)
    else:
        incoming = jnp.concatenate([zero_row, carried[:-1]], axis=0)
    return (local + complex_product(decay_cum, incoming[:, None, :])).reshape(rows, width)


def state_params(nu_part, theta_part, gamma_part):
    modulus = jnp.exp(-jnp.exp(nu_part))
    rotation = jnp.exp(theta_part)
    return (
        modulus * jnp.cos(rotation),
        modulus * jnp.sin(rotation),
        jnp.exp(gamma_part) * jnp.sqrt(1.0 - modulus * modulus),
    )


def contract_rows(left, right):
    return lax.dot_general(
        left, right, (((0,), (0,)), ((), ())), preferred_element_type=jnp.float32
    )


def contract_cols(left, right):
    return lax.dot_general(
        left, right, (((1,), (1,)), ((), ())), preferred_element_type=jnp.float32
    )


def shards(
    block_input,
    segments,
    ln_gain,
    ln_bias,
    b_real,
    b_imag,
    c_real,
    c_imag,
    nu_log,
    theta_log,
    gamma_log,
    d_skip,
    w_value,
    w_gate,
    b_value,
    b_gate,
    out_grad,
):
    tensor_rank = lax.axis_index("tensor")
    (
        gain_all,
        shift_all,
        nu_all,
        theta_all,
        gamma_all,
        skip_all,
        value_bias_all,
        gate_bias_all,
        breal_all,
        bimag_all,
        creal_all,
        cimag_all,
        wvalue_all,
        wgate_all,
    ) = (
        lax.all_gather(ln_gain, "fsdp", axis=0, tiled=True),
        lax.all_gather(ln_bias, "fsdp", axis=0, tiled=True),
        lax.all_gather(nu_log, "fsdp", axis=0, tiled=True),
        lax.all_gather(theta_log, "fsdp", axis=0, tiled=True),
        lax.all_gather(gamma_log, "fsdp", axis=0, tiled=True),
        lax.all_gather(d_skip, "fsdp", axis=0, tiled=True),
        lax.all_gather(b_value, "fsdp", axis=0, tiled=True),
        lax.all_gather(b_gate, "fsdp", axis=0, tiled=True),
        lax.all_gather(b_real, "fsdp", axis=0, tiled=True),
        lax.all_gather(b_imag, "fsdp", axis=0, tiled=True),
        lax.all_gather(c_real, "fsdp", axis=0, tiled=True),
        lax.all_gather(c_imag, "fsdp", axis=0, tiled=True),
        lax.all_gather(w_value, "fsdp", axis=0, tiled=True),
        lax.all_gather(w_gate, "fsdp", axis=0, tiled=True),
    )
    row_count, feature_count = block_input.shape
    group_rows = segments.shape[0]
    state_count = b_real.shape[1]
    unit_count = w_value.shape[1]
    full_states = nu_all.shape[0]
    position = jnp.arange(group_rows)
    earlier_ids = jnp.concatenate([segments[:1], segments[:-1]])
    keep = jnp.where((position % SEQ_LEN > 0) & (segments == earlier_ids), 1.0, 0.0).astype(
        jnp.float32
    )[:, None]
    keep_next = jnp.concatenate([keep[1:], jnp.zeros((1, 1), jnp.float32)], axis=0)
    live = jnp.where(segments > 0, 1.0, 0.0).astype(jnp.float32)[:, None]
    row_live = lax.dynamic_slice_in_dim(live, tensor_rank * row_count, row_count, 0)
    gain = gain_all.astype(jnp.float32)
    shift = shift_all.astype(jnp.float32)
    skip = skip_all.astype(jnp.float32)
    inputs_wide = block_input.astype(jnp.float32)
    centred = inputs_wide - jnp.mean(inputs_wide, axis=1, keepdims=True)
    inverse_std = lax.rsqrt(jnp.mean(centred * centred, axis=1, keepdims=True) + norm_epsilon)
    standard = centred * inverse_std
    normed = (standard * gain + shift).astype(jnp.bfloat16)
    normed_group = lax.all_gather(normed, "tensor", axis=0, tiled=True)
    state_start = tensor_rank * state_count
    (decay_re, decay_im, gamma), params_back = jax.vjp(
        state_params,
        lax.dynamic_slice_in_dim(nu_all.astype(jnp.float32), state_start, state_count),
        lax.dynamic_slice_in_dim(theta_all.astype(jnp.float32), state_start, state_count),
        lax.dynamic_slice_in_dim(gamma_all.astype(jnp.float32), state_start, state_count),
    )
    rate_pair = jnp.concatenate([decay_re, decay_im])
    gamma_pair = jnp.concatenate([gamma, gamma])
    conj_sign = jnp.concatenate(
        [jnp.ones((state_count,), jnp.float32), -jnp.ones((state_count,), jnp.float32)]
    )
    input_pack = jnp.concatenate([breal_all, bimag_all], axis=1)
    output_pack = jnp.concatenate([creal_all, -cimag_all], axis=1)
    drive = jnp.dot(normed_group, input_pack, preferred_element_type=jnp.float32)
    decay = keep * rate_pair
    hidden = blocked_chain(decay, gamma_pair * live * drive, False)
    hidden_low = hidden.astype(jnp.bfloat16)
    state_total = lax.psum_scatter(
        contract_cols(hidden_low, output_pack), "tensor", scatter_dimension=0, tiled=True
    )
    normed_wide = normed.astype(jnp.float32)
    lru_out = state_total + skip * normed_wide
    activated, gelu_back = jax.vjp(jax.nn.gelu, lru_out)
    act = activated.astype(jnp.bfloat16)
    unit_start = tensor_rank * unit_count
    act_group = lax.all_gather(act, "tensor", axis=0, tiled=True)
    value_shift = lax.dynamic_slice_in_dim(
        value_bias_all.astype(jnp.float32), unit_start, unit_count
    )
    gate_shift = lax.dynamic_slice_in_dim(gate_bias_all.astype(jnp.float32), unit_start, unit_count)
    value = jnp.dot(act_group, wvalue_all, preferred_element_type=jnp.float32) + value_shift
    gate = jnp.dot(act_group, wgate_all, preferred_element_type=jnp.float32) + gate_shift
    opening = jax.nn.sigmoid(gate)
    gated_units = (value * opening).astype(jnp.bfloat16)
    gated_mine = lax.all_to_all(gated_units, "tensor", split_axis=0, concat_axis=1, tiled=True)
    mixed = (inputs_wide + row_live * gated_mine.astype(jnp.float32)).astype(jnp.bfloat16)
    cotangent = out_grad.astype(jnp.float32)
    gated_grad = (row_live * cotangent).astype(jnp.bfloat16)
    gated_grad_units = lax.all_to_all(
        gated_grad, "tensor", split_axis=1, concat_axis=0, tiled=True
    ).astype(jnp.float32)
    value_grad = (gated_grad_units * opening).astype(jnp.bfloat16)
    gate_grad = (gated_grad_units * value * opening * (1.0 - opening)).astype(jnp.bfloat16)
    value_weight_grad = contract_rows(act_group, value_grad)
    gate_weight_grad = contract_rows(act_group, gate_grad)
    value_bias_grad = lax.dynamic_update_slice(
        jnp.zeros((feature_count,), jnp.float32),
        jnp.sum(value_grad.astype(jnp.float32), axis=0),
        (unit_start,),
    )
    gate_bias_grad = lax.dynamic_update_slice(
        jnp.zeros((feature_count,), jnp.float32),
        jnp.sum(gate_grad.astype(jnp.float32), axis=0),
        (unit_start,),
    )
    act_grad = lax.psum_scatter(
        contract_cols(value_grad, wvalue_all) + contract_cols(gate_grad, wgate_all),
        "tensor",
        scatter_dimension=0,
        tiled=True,
    )
    lru_grad = gelu_back(act_grad)[0].astype(jnp.bfloat16)
    lru_grad_wide = lru_grad.astype(jnp.float32)
    skip_grad = jnp.sum(lru_grad_wide * normed_wide, axis=0)
    lru_grad_group = lax.all_gather(lru_grad, "tensor", axis=0, tiled=True)
    state_grad = jnp.dot(lru_grad_group, output_pack, preferred_element_type=jnp.float32)
    output_pack_grad = contract_rows(lru_grad_group, hidden_low)
    next_decay = keep_next * (rate_pair * conj_sign)
    total_grad = blocked_chain(next_decay, state_grad, True)
    rate_grad = jnp.sum(keep[1:] * complex_product(hidden[:-1] * conj_sign, total_grad[1:]), axis=0)
    gamma_terms = jnp.sum(live * drive * total_grad, axis=0)
    nu_part_grad, theta_part_grad, gamma_part_grad = params_back(
        (
            rate_grad[:state_count],
            rate_grad[state_count:],
            gamma_terms[:state_count] + gamma_terms[state_count:],
        )
    )
    empty_states = jnp.zeros((full_states,), jnp.float32)
    nu_grad = lax.dynamic_update_slice(empty_states, nu_part_grad, (state_start,))
    theta_grad = lax.dynamic_update_slice(empty_states, theta_part_grad, (state_start,))
    gamma_grad = lax.dynamic_update_slice(empty_states, gamma_part_grad, (state_start,))
    drive_grad = (gamma_pair * live * total_grad).astype(jnp.bfloat16)
    input_pack_grad = contract_rows(normed_group, drive_grad)
    state_part = lax.psum_scatter(
        contract_cols(drive_grad, input_pack).astype(jnp.bfloat16),
        "tensor",
        scatter_dimension=0,
        tiled=True,
    ).astype(jnp.float32)
    normed_grad = state_part + lru_grad_wide * skip
    standard_grad = normed_grad * gain
    gain_grad = jnp.sum(normed_grad * standard, axis=0)
    shift_grad = jnp.sum(normed_grad, axis=0)
    input_grad = cotangent + inverse_std * (
        standard_grad
        - jnp.mean(standard_grad, axis=1, keepdims=True)
        - standard * jnp.mean(standard_grad * standard, axis=1, keepdims=True)
    )
    summed = (
        lax.psum_scatter(gain_grad, "fsdp", scatter_dimension=0, tiled=True),
        lax.psum_scatter(shift_grad, "fsdp", scatter_dimension=0, tiled=True),
        lax.psum_scatter(nu_grad, "fsdp", scatter_dimension=0, tiled=True),
        lax.psum_scatter(theta_grad, "fsdp", scatter_dimension=0, tiled=True),
        lax.psum_scatter(gamma_grad, "fsdp", scatter_dimension=0, tiled=True),
        lax.psum_scatter(skip_grad, "fsdp", scatter_dimension=0, tiled=True),
        lax.psum_scatter(value_bias_grad, "fsdp", scatter_dimension=0, tiled=True),
        lax.psum_scatter(gate_bias_grad, "fsdp", scatter_dimension=0, tiled=True),
        lax.psum_scatter(input_pack_grad[:, :state_count], "fsdp", scatter_dimension=0, tiled=True),
        lax.psum_scatter(input_pack_grad[:, state_count:], "fsdp", scatter_dimension=0, tiled=True),
        lax.psum_scatter(
            output_pack_grad[:, :state_count], "fsdp", scatter_dimension=0, tiled=True
        ),
        lax.psum_scatter(
            -output_pack_grad[:, state_count:], "fsdp", scatter_dimension=0, tiled=True
        ),
        lax.psum_scatter(value_weight_grad, "fsdp", scatter_dimension=0, tiled=True),
        lax.psum_scatter(gate_weight_grad, "fsdp", scatter_dimension=0, tiled=True),
    )
    vectors = lax.psum(
        (summed[0], summed[1], summed[2], summed[3], summed[4], summed[5], summed[6], summed[7]),
        "tensor",
    )
    return (
        mixed,
        input_grad,
        vectors[0],
        vectors[1],
        summed[8],
        summed[9],
        summed[10],
        summed[11],
        vectors[2],
        vectors[3],
        vectors[4],
        vectors[5],
        summed[12],
        summed[13],
        vectors[6],
        vectors[7],
    )


def solution(mesh):
    in_specs = (
        P(("fsdp", "tensor"), None),
        P("fsdp"),
        P("fsdp"),
        P("fsdp"),
        P("fsdp", "tensor"),
        P("fsdp", "tensor"),
        P("fsdp", "tensor"),
        P("fsdp", "tensor"),
        P("fsdp"),
        P("fsdp"),
        P("fsdp"),
        P("fsdp"),
        P("fsdp", "tensor"),
        P("fsdp", "tensor"),
        P("fsdp"),
        P("fsdp"),
        P(("fsdp", "tensor"), None),
    )
    out_specs = (
        P(("fsdp", "tensor"), None),
        P(("fsdp", "tensor"), None),
        P("fsdp"),
        P("fsdp"),
        P("fsdp", "tensor"),
        P("fsdp", "tensor"),
        P("fsdp", "tensor"),
        P("fsdp", "tensor"),
        P("fsdp"),
        P("fsdp"),
        P("fsdp"),
        P("fsdp"),
        P("fsdp", "tensor"),
        P("fsdp", "tensor"),
        P("fsdp"),
        P("fsdp"),
    )
    return jax.shard_map(shards, mesh=mesh, in_specs=in_specs, out_specs=out_specs, check_vma=False)
```

profile of v0, /device:TPU:0, one launch (start us, length us, event | category | flops | bytes accessed | tf_op | source)
XLA Modules:
  0.0 1045.8 jit_solution(13006507848595677849)
XLA Ops:
  16.7 23.9 %all-reduce.52 = (bf16[512]{0:T(512)(128)(2,1)}, bf16[512]{0:T(512)(128)(2,1)}, bf16[256]{0:T(256)(128)(2,1)S(1)}, bf16[256]{0:T(256)(128)(2,1)S(1)}, bf16[512]{...) all-reduce(bf16[512]{0:T(512)(128)(2,1)S(1)} %dynamic-update-slice., ...), channel_id=1, replica_groups=mesh['fsdp'=8,'tensor'=4] {'fsdp'}, use_global_device_ids=true, to_apply=%add.40 | all-reduce | flops 3328 | bytes 13312
  48.2 30.5 %all_gather.60 = bf16[512,64]{1,0:T(8,128)(2,1)S(1)} all-gather(bf16[64,64]{1,0:T(8,128)(2,1)S(1)} %copy-done.229), channel_id=1, replica_groups=mesh['fsdp'=8,'tensor'=4] {'fsdp'}, dimensions={0}, use_global_device_ids=true | all-gather | bytes 73728 | tf_op jit(solution)/shard_map/all_gather | solution.py:132
  78.8 32.5 %all_gather.56 = bf16[512,64]{1,0:T(8,128)(2,1)} all-gather(bf16[64,64]{1,0:T(8,128)(2,1)S(1)} %copy-done.230), channel_id=1, replica_groups=mesh['fsdp'=8,'tensor'=4] {'fsdp'}, dimensions={0}, use_global_device_ids=true | all-gather | bytes 73728 | tf_op jit(solution)/shard_map/all_gather | solution.py:129
  111.3 32.5 %all_gather.57 = bf16[512,64]{1,0:T(8,128)(2,1)} all-gather(bf16[64,64]{1,0:T(8,128)(2,1)S(1)} %copy-done.231), channel_id=1, replica_groups=mesh['fsdp'=8,'tensor'=4] {'fsdp'}, dimensions={0}, use_global_device_ids=true | all-gather | bytes 73728 | tf_op jit(solution)/shard_map/all_gather | solution.py:130
  143.8 30.5 %all_gather.59 = bf16[512,64]{1,0:T(8,128)(2,1)S(1)} all-gather(bf16[64,64]{1,0:T(8,128)(2,1)S(1)} %copy-done.232), channel_id=1, replica_groups=mesh['fsdp'=8,'tensor'=4] {'fsdp'}, dimensions={0}, use_global_device_ids=true | all-gather | bytes 73728 | tf_op jit(solution)/shard_map/all_gather | solution.py:131
  175.2 2.3 broadcast_multiply_fusion
  190.3 5.0 multiply_multiply_fusion.3
  195.3 2.5 fusion.98
  214.0 2.6 copy.194
  216.5 6.0 stack.153
  225.0 4.6 fusion.39
  230.3 68.5 %reduce-scatter.18.cloned.1.call-done = f32[1024,512]{1,0:T(8,128)} async-done(((f32[4096,512]{1,0:T(8,128)}), f32[1024,512]{1,0:T(8,128)}) %reduce-scatter.18.cloned.1.call-update) | async-done | bytes 2097168 | tf_op jit(solution)/shard_map/reduce_scatter | solution.py:176
  298.8 3.5 multiply_convert_fusion.1
  302.4 2.6 copy_bitcast_fusion
  304.9 4.2 all-to-all-start.1
  309.4 30.6 %all_gather.63 = bf16[512,128]{1,0:T(8,128)(2,1)S(1)} all-gather(bf16[64,128]{1,0:T(8,128)(2,1)S(1)} %copy-done.233), channel_id=1, replica_groups=mesh['fsdp'=8,'tensor'=4] {'fsdp'}, dimensions={0}, use_global_device_ids=true | all-gather | bytes 147456 | tf_op jit(solution)/shard_map/all_gather | solution.py:133
  340.1 30.5 %all_gather.65 = bf16[512,128]{1,0:T(8,128)(2,1)S(1)} all-gather(bf16[64,128]{1,0:T(8,128)(2,1)S(1)} %copy-done.234), channel_id=1, replica_groups=mesh['fsdp'=8,'tensor'=4] {'fsdp'}, dimensions={0}, use_global_device_ids=true | all-gather | bytes 147456 | tf_op jit(solution)/shard_map/all_gather | solution.py:134
  370.6 4.8 convolution_add_fusion.2
  375.4 6.0 convert_reduce_fusion.1
  382.8 4.6 convolution_add_fusion
  387.4 73.1 %reduce-scatter.20.cloned.1.call-done = f32[1024,512]{1,0:T(8,128)} async-done(((f32[4096,512]{1,0:T(8,128)}), f32[1024,512]{1,0:T(8,128)}) %reduce-scatter.20.cloned.1.call-update) | async-done | bytes 2097168 | tf_op jit(solution)/shard_map/reduce_scatter | solution.py:214
  460.5 4.5 fusion.28
  465.4 2.5 fusion.97
  480.0 19.6 %all-gather.8.cloned.1.call-done = bf16[4096,512]{1,0:T(8,128)(2,1)} async-done(((bf16[1024,512]{1,0:T(8,128)(2,1)}), bf16[4096,512]{1,0:T(8,128)(2,1)}) %all-gather.8.cloned.1.call-update) | async-done | bytes 4194320 | tf_op jit(solution)/shard_map/all_gather | solution.py:223
  499.6 3.6 fusion.71
  503.2 2.4 fusion.96
  580.6 2.5 copy.229
  583.1 7.8 stack.171
  591.0 3.0 multiply_subtract_fusion.1
  597.7 3.0 convolution_convert_fusion
  602.1 4.5 fusion.108
  608.1 4.4 all-to-all-start
  613.6 4.5 fusion.109
  618.2 3.7 fusion.37
  622.8 6.8 multiply_subtract_fusion
  630.7 3.8 fusion.90
  636.5 2.9 fusion.30
  640.8 10.1 reduce-scatter.22.cloned.1.call-done
  650.8 2.9 fusion.15
  653.7 37.2 %all-reduce.50 = (f32[512]{0:T(512)S(1)}, f32[512]{0:T(512)S(1)}, f32[256]{0:T(256)S(1)}, f32[256]{0:T(256)S(1)}, f32[256]{0:T(256)S(1)}, /*index=5*/f32[512]{0:T(512)S(1)}, f32[512]{0:T(512)S(1)}, f32[512]{0:T(512)S(1)}) all-reduce(f32[512]{0:T(512)S(1)} %get-tuple-element.64, ...), channel_id=5, replica_groups=mesh['fsdp'=8,'tensor'=4] {'fsdp'}, use_global_device_ids=true, to_apply=%region_8.9.clone | all-reduce | flops 3328 | bytes 26624
  691.5 6.3 all-reduce.51
  697.8 3.8 convert_add_fusion.1
  701.6 14.8 %reduce-scatter.24.cloned.1.call-done = f32[64,128]{1,0:T(8,128)} async-done(((f32[512,128]{1,0:T(8,128)}), f32[64,128]{1,0:T(8,128)}) %reduce-scatter.24.cloned.1.call-update) | async-done | bytes 32784 | tf_op jit(solution)/shard_map/reduce_scatter | solution.py:275
  716.3 64.5 %reduce-scatter.26.cloned.1.call-done = f32[64,128]{1,0:T(8,128)} async-done(((f32[512,128]{1,0:T(8,128)}), f32[64,128]{1,0:T(8,128)}) %reduce-scatter.26.cloned.1.call-update) | async-done | bytes 32784 | tf_op jit(solution)/shard_map/reduce_scatter | solution.py:276
  780.8 64.5 %reduce-scatter.34.cloned.1.call-done = f32[64,64]{1,0:T(8,128)} async-done(((f32[512,64]{1,0:T(8,128)}), f32[64,64]{1,0:T(8,128)}) %reduce-scatter.34.cloned.1.call-update) | async-done | bytes 16400
  845.3 64.4 %reduce-scatter.32.cloned.1.call-done = f32[64,64]{1,0:T(8,128)} async-done(((f32[512,64]{1,0:T(8,128)}), f32[64,64]{1,0:T(8,128)}) %reduce-scatter.32.cloned.1.call-update) | async-done | bytes 16400
  909.7 64.5 %reduce-scatter.30.cloned.1.call-done = f32[64,64]{1,0:T(8,128)} async-done(((f32[512,64]{1,0:T(8,128)}), f32[64,64]{1,0:T(8,128)}) %reduce-scatter.30.cloned.1.call-update) | async-done | bytes 16400
  974.3 64.4 %reduce-scatter.28.cloned.1.call-done = f32[64,64]{1,0:T(8,128)} async-done(((f32[512,64]{1,0:T(8,128)}), f32[64,64]{1,0:T(8,128)}) %reduce-scatter.28.cloned.1.call-update) | async-done | bytes 16400
  (985 shorter events, 146.3 us)
Async XLA Ops:
  7.2 37.3 %copy-start = (bf16[1024,512]{1,0:T(8,128)(2,1)S(1)}, bf16[1024,512]{1,0:T(8,128)(2,1)}, u32[]{:S(2)}) copy-start(bf16[1024,512]{1,0:T(8,128)(2,1)} %param.17) | copy-start | bytes 3145732
  7.2 183.1 %all-gather.4.cloned.1.call-start = ((), (), s32[]{:S(2)}) async-start(), calls=%async_computation.11 | async-start | bytes 5242880 | tf_op jit(solution)/shard_map/all_gather | solution.py:157
  44.4 34.3 %copy-start.230 = (bf16[64,64]{1,0:T(8,128)(2,1)S(1)}, bf16[64,64]{1,0:T(8,128)(2,1)}, u32[]{:S(2)}) copy-start(bf16[64,64]{1,0:T(8,128)(2,1)} %param.21) | copy-start | bytes 24580
  44.4 66.8 %copy-start.231 = (bf16[64,64]{1,0:T(8,128)(2,1)S(1)}, bf16[64,64]{1,0:T(8,128)(2,1)}, u32[]{:S(2)}) copy-start(bf16[64,64]{1,0:T(8,128)(2,1)} %param.22) | copy-start | bytes 24580
  44.4 99.4 %copy-start.232 = (bf16[64,64]{1,0:T(8,128)(2,1)S(1)}, bf16[64,64]{1,0:T(8,128)(2,1)}, u32[]{:S(2)}) copy-start(bf16[64,64]{1,0:T(8,128)(2,1)} %param.23) | copy-start | bytes 24580
  44.4 130.7 %copy-start.249 = (f32[128]{0:T(128)S(1)}, f32[128]{0:T(128)}, u32[]{:S(2)}) copy-start(f32[128]{0:T(128)} %constant.70.clone.1) | copy-start | bytes 1540
  45.9 252.9 %reduce-scatter.18.cloned.1.call-start = ((), (), s32[]{:S(2)}) async-start(), calls=%async_computation.12 | async-start | bytes 10485760 | tf_op jit(solution)/shard_map/reduce_scatter | solution.py:176
  47.4 130.2 %copy-start.245 = (f32[256]{0:T(256)}, f32[256]{0:T(256)S(1)}, u32[]{:S(2)}) copy-start(f32[256]{0:T(256)S(1)} %convert_element_type.102) | copy-start | bytes 3076
  47.4 130.1 %copy-start.247 = (f32[256]{0:T(256)}, f32[256]{0:T(256)S(1)}, u32[]{:S(2)}) copy-start(f32[256]{0:T(256)S(1)} %convert_element_type.97) | copy-start | bytes 3076
  47.4 130.1 %copy-start.251 = (f32[256]{0:T(256)}, f32[256]{0:T(256)S(1)}, u32[]{:S(2)}) copy-start(f32[256]{0:T(256)S(1)} %convert_element_type.98) | copy-start | bytes 3076
  78.8 146.2 %copy-start.36 = (bf16[512,64]{1,0:T(8,128)(2,1)}, bf16[512,64]{1,0:T(8,128)(2,1)S(1)}, u32[]{:S(2)}) copy-start(bf16[512,64]{1,0:T(8,128)(2,1)S(1)} %neg.22) | copy-start | bytes 196612
  174.3 50.6 %copy-start.37 = (bf16[512,64]{1,0:T(8,128)(2,1)}, bf16[512,64]{1,0:T(8,128)(2,1)S(1)}, u32[]{:S(2)}) copy-start(bf16[512,64]{1,0:T(8,128)(2,1)S(1)} %all_gather.59) | copy-start | bytes 196612
  179.8 9.8 copy-start.38
  229.6 69.2 %copy-start.212 = (f32[1024]{0:T(1024)S(1)}, f32[1024]{0:T(1024)}, u32[]{:S(2)}) copy-start(f32[1024]{0:T(1024)} %copy-done.211) | copy-start | bytes 12292
  229.6 69.2 %copy-start.215 = (f32[1024]{0:T(1024)S(1)}, f32[1024]{0:T(1024)}, u32[]{:S(2)}) copy-start(f32[1024]{0:T(1024)} %copy-done.214) | copy-start | bytes 12292
  229.6 69.2 %copy-start.219 = (f32[512]{0:T(512)S(1)}, f32[512]{0:T(512)}, u32[]{:S(2)}) copy-start(f32[512]{0:T(512)} %copy-done.218) | copy-start | bytes 6148
  229.6 69.2 %copy-start.225 = (f32[512]{0:T(512)S(1)}, f32[512]{0:T(512)}, u32[]{:S(2)}) copy-start(f32[512]{0:T(512)} %copy-done.224) | copy-start | bytes 6148
  229.6 140.9 %all-gather.6.cloned.1.call-start = ((), (), s32[]{:S(2)}) async-start(), calls=%async_computation.13 | async-start | bytes 5242880 | tf_op jit(solution)/shard_map/all_gather | solution.py:184
  230.3 230.2 %copy-start.222 = (f32[512]{0:T(512)}, f32[512]{0:T(512)S(1)}, u32[]{:S(2)}) copy-start(f32[512]{0:T(512)S(1)} %convert_element_type.104) | copy-start | bytes 6148
  302.4 37.7 %copy-start.234 = (bf16[64,128]{1,0:T(8,128)(2,1)S(1)}, bf16[64,128]{1,0:T(8,128)(2,1)}, u32[]{:S(2)}) copy-start(bf16[64,128]{1,0:T(8,128)(2,1)} %param.30) | copy-start | bytes 49156
  304.9 70.4 %all-to-all-start.1 = ((bf16[1024,4,128]{2,0,1:T(8,128)(2,1)}), bf16[1024,4,128]{2,0,1:T(8,128)(2,1)}, u32[]{:S(2)}, u32[]{:S(2)}) async-start(bf16[1024,4,128]{2,0,1:T(8,128)(2,1)} %copy_bitcast_fusion), calls=%async_computation.2 | async-start | bytes 2097152 | tf_op jit(solution)/shard_map/all_to_all | solution.py:197
  309.2 151.3 %reduce-scatter.20.cloned.1.call-start = ((), (), s32[]{:S(2)}) async-start(), calls=%async_computation.14 | async-start | bytes 10485760 | tf_op jit(solution)/shard_map/reduce_scatter | solution.py:214
  387.4 112.3 %all-gather.8.cloned.1.call-start = ((), (), s32[]{:S(2)}) async-start(), calls=%async_computation.15 | async-start | bytes 5242880 | tf_op jit(solution)/shard_map/all_gather | solution.py:223
  465.0 185.8 %reduce-scatter.22.cloned.1.call-start = ((), (), s32[]{:S(2)}) async-start(), calls=%async_computation.16 | async-start | bytes 5242880 | tf_op jit(solution)/shard_map/reduce_scatter | solution.py:243
  469.5 9.8 copy-start.40
  469.5 9.8 copy-start.42
  511.6 21.8 %copy-start.102 = (f32[256,64]{1,0:T(8,128)}, f32[256,64]{1,0:T(8,128)S(1)}, u32[]{:S(2)}) copy-start(f32[256,64]{1,0:T(8,128)S(1)} %get-tuple-element.248) | copy-start | bytes 196612
  523.5 28.1 %copy-start.205 = (f32[127,128]{1,0:T(8,128)S(1)}, f32[127,128]{1,0:T(8,128)}, u32[]{:S(2)}) copy-start(f32[127,128]{1,0:T(8,128)} %slice.1920) | copy-start | bytes 195076
  534.0 20.2 %copy-start.210 = (f32[127,128]{1,0:T(8,128)S(1)}, f32[127,128]{1,0:T(8,128)}, u32[]{:S(2)}) copy-start(f32[127,128]{1,0:T(8,128)} %slice.2051) | copy-start | bytes 195076
  570.0 9.2 copy-start.65
  600.7 115.6 %reduce-scatter.24.cloned.1.call-start = ((), (), s32[]{:S(2)}) async-start(), calls=%async_computation.17 | async-start | bytes 294912 | tf_op jit(solution)/shard_map/reduce_scatter | solution.py:275
  608.1 89.7 %all-to-all-start = ((bf16[4,1024,128]{2,1,0:T(8,128)(2,1)}), bf16[4,1024,128]{2,1,0:T(8,128)(2,1)}, u32[]{:S(2)}, u32[]{:S(2)}) async-start(bf16[4,1024,128]{2,1,0:T(8,128)(2,1)} %bitcast.520), calls=%async_computation.1 | async-start | bytes 2097152 | tf_op jit(solution)/shard_map/all_to_all | solution.py:193
  612.5 168.3 %reduce-scatter.26.cloned.1.call-start = ((), (), s32[]{:S(2)}) async-start(), calls=%async_computation.18 | async-start | bytes 294912 | tf_op jit(solution)/shard_map/reduce_scatter | solution.py:276
  618.1 227.2 %reduce-scatter.34.cloned.1.call-start = ((), (), s32[]{:S(2)}) async-start(), calls=%async_computation.22 | async-start | bytes 294912
  622.8 8.0 copy-start.2
  622.8 287.0 %reduce-scatter.32.cloned.1.call-start = ((), (), s32[]{:S(2)}) async-start(), calls=%async_computation.21 | async-start | bytes 294912
  630.5 343.8 %reduce-scatter.30.cloned.1.call-start = ((), (), s32[]{:S(2)}) async-start(), calls=%async_computation.20 | async-start | bytes 294912
  636.3 402.4 %reduce-scatter.28.cloned.1.call-start = ((), (), s32[]{:S(2)}) async-start(), calls=%async_computation.19 | async-start | bytes 294912
  636.4 14.4 %copy-start.3 = (bf16[1024,512]{1,0:T(8,128)(2,1)S(1)}, bf16[1024,512]{1,0:T(8,128)(2,1)}, u32[]{:S(2)}) copy-start(bf16[1024,512]{1,0:T(8,128)(2,1)} %fusion.28) | copy-start | bytes 3145732
  636.4 14.4 %copy-start.213 = (f32[1024]{0:T(1024)S(1)}, f32[1024]{0:T(1024)}, u32[]{:S(2)}) copy-start(f32[1024]{0:T(1024)} %copy-done.211) | copy-start | bytes 12292
  636.4 14.4 %copy-start.216 = (f32[1024]{0:T(1024)S(1)}, f32[1024]{0:T(1024)}, u32[]{:S(2)}) copy-start(f32[1024]{0:T(1024)} %copy-done.214) | copy-start | bytes 12292
  636.4 14.4 %copy-start.220 = (f32[512]{0:T(512)S(1)}, f32[512]{0:T(512)}, u32[]{:S(2)}) copy-start(f32[512]{0:T(512)} %copy-done.218) | copy-start | bytes 6148
  636.5 14.4 %copy-start.223 = (f32[512]{0:T(512)S(1)}, f32[512]{0:T(512)}, u32[]{:S(2)}) copy-start(f32[512]{0:T(512)} %copy-done.222) | copy-start | bytes 6148
  636.5 14.4 %copy-start.226 = (f32[512]{0:T(512)S(1)}, f32[512]{0:T(512)}, u32[]{:S(2)}) copy-start(f32[512]{0:T(512)} %copy-done.224) | copy-start | bytes 6148
  639.4 14.4 %copy-start.241 = (f32[512]{0:T(512)S(1)}, f32[512]{0:T(512)}, u32[]{:S(2)}) copy-start(f32[512]{0:T(512)} %copy-done.240) | copy-start | bytes 6148
  639.4 14.4 %copy-start.243 = (f32[512]{0:T(512)S(1)}, f32[512]{0:T(512)}, u32[]{:S(2)}) copy-start(f32[512]{0:T(512)} %copy-done.242) | copy-start | bytes 6148
  639.4 58.4 %copy-start.8 = (bf16[1024,512]{1,0:T(8,128)(2,1)S(1)}, bf16[1024,512]{1,0:T(8,128)(2,1)}, u32[]{:S(2)}) copy-start(bf16[1024,512]{1,0:T(8,128)(2,1)} %param.33) | copy-start | bytes 3145732
  639.4 58.4 %copy-start.228 = (f32[1024]{0:T(1024)S(1)}, f32[1024]{0:T(1024)}, u32[]{:S(2)}) copy-start(f32[1024]{0:T(1024)} %copy-done.227) | copy-start | bytes 12292
  (224 other events, 562.5 us)
Sparse Core Ops, SparseCore 0:
  46.0 31.7 all-gather.3
  229.8 68.9 reduce-scatter.17
  302.4 45.2 all-gather.5
  387.5 72.9 reduce-scatter.19
  465.1 34.4 all-gather.7
  600.8 49.9 reduce-scatter.21
  655.1 61.2 reduce-scatter.23
  720.6 60.1 reduce-scatter.25
  785.1 60.2 reduce-scatter.33
  849.5 60.2 reduce-scatter.31
  914.0 60.2 reduce-scatter.29
  978.4 60.2 reduce-scatter.27
where the time goes:
time: 1050 us
  waiting for transfers between devices  509 us (48%)
  blocking collectives  255 us (24%)
  other arithmetic  114 us (11%)
  local copies, waits for them, and re-layouts  88 us (8%)
  matrix products  49.3 us (5%)
  between operations  21.5 us (2%)
    unnamed x16, waiting for transfers between devices  258 us
    reduce_scatter x1, waiting for transfers between devices, shards(): lax.psum_scatter(contract_cols(value_grad, wvalue_all) + contract_cols(ga...  73.1 us
    reduce_scatter x1, waiting for transfers between devices, shards(): lax.psum_scatter(contract_cols(hidden_low, output_pack), 'tensor', scatte...  68.5 us
    reduce_scatter x1, waiting for transfers between devices, shards(): lax.psum_scatter(gate_weight_grad, 'fsdp', scatter_dimension=0, tiled=True)  64.5 us
    unnamed x2, blocking collectives  61.1 us
    all_gather x1, blocking collectives, shards(): lax.all_gather(b_imag, 'fsdp', axis=0, tiled=True)  32.5 us
    all_gather x1, blocking collectives, shards(): lax.all_gather(b_real, 'fsdp', axis=0, tiled=True)  32.5 us
    all_gather x1, blocking collectives, shards(): lax.all_gather(w_value, 'fsdp', axis=0, tiled=True)  30.6 us
  transfers between devices with their start and end apart: 14, of which 10 were waited for; matrix products, arithmetic and copies ran while one was open for 8% of the time, Pallas kernels for 0%

commit v1 on v0

--- a/solution.py
+++ b/solution.py
@@ -126,7 +126,9 @@
         lax.all_gather(d_skip, "fsdp", axis=0, tiled=True),
         lax.all_gather(b_value, "fsdp", axis=0, tiled=True),
         lax.all_gather(b_gate, "fsdp", axis=0, tiled=True),
-        lax.all_gather(b_real, "fsdp", axis=0, tiled=True),
+        jnp.concatenate(
+            lax.all_to_all(jnp.stack([b_real] * lax.axis_size("fsdp")), "fsdp", 0, 0), axis=0
+        ),
         lax.all_gather(b_imag, "fsdp", axis=0, tiled=True),
         lax.all_gather(c_real, "fsdp", axis=0, tiled=True),
         lax.all_gather(c_imag, "fsdp", axis=0, tiled=True),

time: 1050 us -> 1030 us (0.981)
  blocking collectives: 255 us -> 222 us
    all_gather x1 -> x0, blocking collectives: 32.5 us -> none  [shards(): lax.all_gather(b_real, 'fsdp', axis=0, tiled=True)]
    unnamed x548 -> x552, local copies, waits for them, and re-layouts: 20.3 us -> 22 us
  transfers between devices with their start and end apart: 14 -> 15, of which waited for: 10 -> 10; matrix products, arithmetic and copies ran while one was open for 8% -> 8% of each run, Pallas kernels for 0% -> 0%
where the time goes in v1:
time: 1030 us; the launch traced here: 1020 us
  waiting for transfers between devices  512 us (50%)
  blocking collectives  222 us (22%)
  other arithmetic  114 us (11%)
  local copies, waits for them, and re-layouts  89.7 us (9%)
  matrix products  49.3 us (5%)
  between operations  21.6 us (2%)
  starting transfers between devices  13.8 us (1%)
    unnamed x16, waiting for transfers between devices  258 us
    reduce_scatter x1, waiting for transfers between devices, shards(): lax.psum_scatter(contract_cols(value_grad, wvalue_all) + contract_cols(ga...  73 us
    reduce_scatter x1, waiting for transfers between devices, shards(): lax.psum_scatter(contract_cols(hidden_low, output_pack), 'tensor', scatte...  72.1 us
    reduce_scatter x1, waiting for transfers between devices, shards(): lax.psum_scatter(gate_weight_grad, 'fsdp', scatter_dimension=0, tiled=True)  64.6 us
    unnamed x2, blocking collectives  61.1 us
    all_gather x1, blocking collectives, shards(): lax.all_gather(b_imag, 'fsdp', axis=0, tiled=True)  32.2 us
    all_gather x1, blocking collectives, shards(): lax.all_gather(c_imag, 'fsdp', axis=0, tiled=True)  31 us
    all_gather x1, blocking collectives, shards(): lax.all_gather(w_value, 'fsdp', axis=0, tiled=True)  30.7 us
  transfers between devices with their start and end apart: 15, of which 10 were waited for; matrix products, arithmetic and copies ran while one was open for 8% of the time, Pallas kernels for 0%

profile of v1, /device:TPU:0, one launch (start us, length us, event | category | flops | bytes accessed | tf_op | source)
XLA Modules:
  0.0 1023.4 jit_solution(1246289665687001657)
XLA Ops:
  16.7 23.9 %all-reduce.52 = (bf16[512]{0:T(512)(128)(2,1)}, bf16[512]{0:T(512)(128)(2,1)}, bf16[256]{0:T(256)(128)(2,1)S(1)}, bf16[256]{0:T(256)(128)(2,1)S(1)}, bf16[512]{...) all-reduce(bf16[512]{0:T(512)(128)(2,1)S(1)} %dynamic-update-slice., ...), channel_id=1, replica_groups=mesh['fsdp'=8,'tensor'=4] {'fsdp'}, use_global_device_ids=true, to_apply=%add.40 | all-reduce | flops 3328 | bytes 13312
  46.7 4.0 all-to-all-start
  53.0 31.0 %all_gather.56 = bf16[512,64]{1,0:T(8,128)(2,1)S(1)} all-gather(bf16[64,64]{1,0:T(8,128)(2,1)S(1)} %copy-done.231), channel_id=1, replica_groups=mesh['fsdp'=8,'tensor'=4] {'fsdp'}, dimensions={0}, use_global_device_ids=true | all-gather | bytes 73728 | tf_op jit(solution)/shard_map/all_gather | solution.py:134
  84.0 32.2 %all_gather.53 = bf16[512,64]{1,0:T(8,128)(2,1)} all-gather(bf16[64,64]{1,0:T(8,128)(2,1)S(1)} %copy-done.232), channel_id=1, replica_groups=mesh['fsdp'=8,'tensor'=4] {'fsdp'}, dimensions={0}, use_global_device_ids=true | all-gather | bytes 73728 | tf_op jit(solution)/shard_map/all_gather | solution.py:132
  116.3 30.6 %all_gather.55 = bf16[512,64]{1,0:T(8,128)(2,1)S(1)} all-gather(bf16[64,64]{1,0:T(8,128)(2,1)S(1)} %copy-done.233), channel_id=1, replica_groups=mesh['fsdp'=8,'tensor'=4] {'fsdp'}, dimensions={0}, use_global_device_ids=true | all-gather | bytes 73728 | tf_op jit(solution)/shard_map/all_gather | solution.py:133
  147.7 2.3 broadcast_multiply_fusion
  163.9 5.0 multiply_multiply_fusion.3
  168.9 2.5 fusion.98
  187.6 2.5 copy.194
  190.2 6.0 stack.165
  198.6 4.7 fusion.39
  203.9 72.1 %reduce-scatter.18.cloned.1.call-done = f32[1024,512]{1,0:T(8,128)} async-done(((f32[4096,512]{1,0:T(8,128)}), f32[1024,512]{1,0:T(8,128)}) %reduce-scatter.18.cloned.1.call-update) | async-done | bytes 2097168 | tf_op jit(solution)/shard_map/reduce_scatter | solution.py:178
  276.0 3.5 multiply_convert_fusion.1
  279.6 2.6 copy_bitcast_fusion
  282.2 4.3 all-to-all-start.2
  286.6 30.7 %all_gather.59 = bf16[512,128]{1,0:T(8,128)(2,1)S(1)} all-gather(bf16[64,128]{1,0:T(8,128)(2,1)S(1)} %copy-done.234), channel_id=1, replica_groups=mesh['fsdp'=8,'tensor'=4] {'fsdp'}, dimensions={0}, use_global_device_ids=true | all-gather | bytes 147456 | tf_op jit(solution)/shard_map/all_gather | solution.py:135
  317.3 30.5 %all_gather.61 = bf16[512,128]{1,0:T(8,128)(2,1)S(1)} all-gather(bf16[64,128]{1,0:T(8,128)(2,1)S(1)} %copy-done.235), channel_id=1, replica_groups=mesh['fsdp'=8,'tensor'=4] {'fsdp'}, dimensions={0}, use_global_device_ids=true | all-gather | bytes 147456 | tf_op jit(solution)/shard_map/all_gather | solution.py:136
  347.8 4.8 convolution_add_fusion.2
  352.6 6.0 convert_reduce_fusion.1
  360.0 4.6 convolution_add_fusion
  364.7 73.0 %reduce-scatter.20.cloned.1.call-done = f32[1024,512]{1,0:T(8,128)} async-done(((f32[4096,512]{1,0:T(8,128)}), f32[1024,512]{1,0:T(8,128)}) %reduce-scatter.20.cloned.1.call-update) | async-done | bytes 2097168 | tf_op jit(solution)/shard_map/reduce_scatter | solution.py:216
  437.7 4.5 fusion.28
  442.7 2.5 fusion.97
  457.3 19.5 %all-gather.8.cloned.1.call-done = bf16[4096,512]{1,0:T(8,128)(2,1)} async-done(((bf16[1024,512]{1,0:T(8,128)(2,1)}), bf16[4096,512]{1,0:T(8,128)(2,1)}) %all-gather.8.cloned.1.call-update) | async-done | bytes 4194320 | tf_op jit(solution)/shard_map/all_gather | solution.py:225
  476.9 3.6 fusion.71
  480.5 2.4 fusion.96
  558.0 2.5 copy.229
  560.5 7.8 stack.183
  568.3 3.0 multiply_subtract_fusion.1
  575.1 3.0 convolution_convert_fusion
  579.5 4.5 fusion.108
  585.5 4.4 all-to-all-start.1
  590.9 4.5 fusion.109
  595.5 3.7 fusion.37
  600.1 6.8 multiply_subtract_fusion
  608.0 3.8 fusion.90
  613.8 2.9 fusion.30
  618.0 10.2 reduce-scatter.22.cloned.1.call-done
  628.2 2.9 fusion.15
  631.1 37.1 %all-reduce.50 = (f32[512]{0:T(512)S(1)}, f32[512]{0:T(512)S(1)}, f32[256]{0:T(256)S(1)}, f32[256]{0:T(256)S(1)}, f32[256]{0:T(256)S(1)}, /*index=5*/f32[512]{0:T(512)S(1)}, f32[512]{0:T(512)S(1)}, f32[512]{0:T(512)S(1)}) all-reduce(f32[512]{0:T(512)S(1)} %get-tuple-element.64, ...), channel_id=5, replica_groups=mesh['fsdp'=8,'tensor'=4] {'fsdp'}, use_global_device_ids=true, to_apply=%region_8.9.clone | all-reduce | flops 3328 | bytes 26624
  668.9 6.3 all-reduce.51
  675.1 3.8 convert_add_fusion.1
  679.0 14.8 %reduce-scatter.24.cloned.1.call-done = f32[64,128]{1,0:T(8,128)} async-done(((f32[512,128]{1,0:T(8,128)}), f32[64,128]{1,0:T(8,128)}) %reduce-scatter.24.cloned.1.call-update) | async-done | bytes 32784 | tf_op jit(solution)/shard_map/reduce_scatter | solution.py:277
  693.7 64.6 %reduce-scatter.26.cloned.1.call-done = f32[64,128]{1,0:T(8,128)} async-done(((f32[512,128]{1,0:T(8,128)}), f32[64,128]{1,0:T(8,128)}) %reduce-scatter.26.cloned.1.call-update) | async-done | bytes 32784 | tf_op jit(solution)/shard_map/reduce_scatter | solution.py:278
  758.3 64.6 %reduce-scatter.34.cloned.1.call-done = f32[64,64]{1,0:T(8,128)} async-done(((f32[512,64]{1,0:T(8,128)}), f32[64,64]{1,0:T(8,128)}) %reduce-scatter.34.cloned.1.call-update) | async-done | bytes 16400
  822.9 64.4 %reduce-scatter.32.cloned.1.call-done = f32[64,64]{1,0:T(8,128)} async-done(((f32[512,64]{1,0:T(8,128)}), f32[64,64]{1,0:T(8,128)}) %reduce-scatter.32.cloned.1.call-update) | async-done | bytes 16400
  887.3 64.6 %reduce-scatter.30.cloned.1.call-done = f32[64,64]{1,0:T(8,128)} async-done(((f32[512,64]{1,0:T(8,128)}), f32[64,64]{1,0:T(8,128)}) %reduce-scatter.30.cloned.1.call-update) | async-done | bytes 16400
  951.9 64.4 %reduce-scatter.28.cloned.1.call-done = f32[64,64]{1,0:T(8,128)} async-done(((f32[512,64]{1,0:T(8,128)}), f32[64,64]{1,0:T(8,128)}) %reduce-scatter.28.cloned.1.call-update) | async-done | bytes 16400
  (991 shorter events, 148.3 us)
Async XLA Ops:
  7.2 37.3 %copy-start = (bf16[1024,512]{1,0:T(8,128)(2,1)S(1)}, bf16[1024,512]{1,0:T(8,128)(2,1)}, u32[]{:S(2)}) copy-start(bf16[1024,512]{1,0:T(8,128)(2,1)} %param.17) | copy-start | bytes 3145732
  7.2 156.7 %all-gather.4.cloned.1.call-start = ((), (), s32[]{:S(2)}) async-start(), calls=%async_computation.12 | async-start | bytes 5242880 | tf_op jit(solution)/shard_map/all_gather | solution.py:159
  42.1 8.7 copy-start.222
  44.4 39.6 %copy-start.232 = (bf16[64,64]{1,0:T(8,128)(2,1)S(1)}, bf16[64,64]{1,0:T(8,128)(2,1)}, u32[]{:S(2)}) copy-start(bf16[64,64]{1,0:T(8,128)(2,1)} %param.22) | copy-start | bytes 24580
  44.5 71.8 %copy-start.233 = (bf16[64,64]{1,0:T(8,128)(2,1)S(1)}, bf16[64,64]{1,0:T(8,128)(2,1)}, u32[]{:S(2)}) copy-start(bf16[64,64]{1,0:T(8,128)(2,1)} %param.23) | copy-start | bytes 24580
  44.5 103.2 %copy-start.250 = (f32[128]{0:T(128)S(1)}, f32[128]{0:T(128)}, u32[]{:S(2)}) copy-start(f32[128]{0:T(128)} %constant.70.clone.1) | copy-start | bytes 1540
  46.7 116.2 %all-to-all-start = ((bf16[8,2,2048]{2,1,0:T(2,128)(2,1)}), bf16[8,2,2048]{2,1,0:T(2,128)(2,1)}, u32[]{:S(2)}, u32[]{:S(2)}) async-start(bf16[8,2,2048]{2,1,0:T(2,128)(2,1)} %reshape.259), calls=%async_computation | async-start | bytes 131072 | tf_op jit(solution)/shard_map/all_to_all | solution.py:130
  50.7 225.3 %reduce-scatter.18.cloned.1.call-start = ((), (), s32[]{:S(2)}) async-start(), calls=%async_computation.13 | async-start | bytes 10485760 | tf_op jit(solution)/shard_map/reduce_scatter | solution.py:178
  52.2 97.8 %copy-start.246 = (f32[256]{0:T(256)}, f32[256]{0:T(256)S(1)}, u32[]{:S(2)}) copy-start(f32[256]{0:T(256)S(1)} %convert_element_type.102) | copy-start | bytes 3076
  52.2 97.8 %copy-start.248 = (f32[256]{0:T(256)}, f32[256]{0:T(256)S(1)}, u32[]{:S(2)}) copy-start(f32[256]{0:T(256)S(1)} %convert_element_type.97) | copy-start | bytes 3076
  52.3 97.8 %copy-start.252 = (f32[256]{0:T(256)}, f32[256]{0:T(256)S(1)}, u32[]{:S(2)}) copy-start(f32[256]{0:T(256)S(1)} %convert_element_type.98) | copy-start | bytes 3076
  84.0 114.6 %copy-start.36 = (bf16[512,64]{1,0:T(8,128)(2,1)}, bf16[512,64]{1,0:T(8,128)(2,1)S(1)}, u32[]{:S(2)}) copy-start(bf16[512,64]{1,0:T(8,128)(2,1)S(1)} %neg.22) | copy-start | bytes 196612
  146.8 51.8 %copy-start.37 = (bf16[512,64]{1,0:T(8,128)(2,1)}, bf16[512,64]{1,0:T(8,128)(2,1)S(1)}, u32[]{:S(2)}) copy-start(bf16[512,64]{1,0:T(8,128)(2,1)S(1)} %all_gather.55) | copy-start | bytes 196612
  152.3 9.8 copy-start.38
  203.2 72.8 %copy-start.213 = (f32[1024]{0:T(1024)S(1)}, f32[1024]{0:T(1024)}, u32[]{:S(2)}) copy-start(f32[1024]{0:T(1024)} %copy-done.212) | copy-start | bytes 12292
  203.2 72.8 %copy-start.216 = (f32[1024]{0:T(1024)S(1)}, f32[1024]{0:T(1024)}, u32[]{:S(2)}) copy-start(f32[1024]{0:T(1024)} %copy-done.215) | copy-start | bytes 12292
  203.2 72.8 %copy-start.220 = (f32[512]{0:T(512)S(1)}, f32[512]{0:T(512)}, u32[]{:S(2)}) copy-start(f32[512]{0:T(512)} %copy-done.219) | copy-start | bytes 6148
  203.2 72.8 %copy-start.226 = (f32[512]{0:T(512)S(1)}, f32[512]{0:T(512)}, u32[]{:S(2)}) copy-start(f32[512]{0:T(512)} %copy-done.225) | copy-start | bytes 6148
  203.3 144.5 %all-gather.6.cloned.1.call-start = ((), (), s32[]{:S(2)}) async-start(), calls=%async_computation.14 | async-start | bytes 5242880 | tf_op jit(solution)/shard_map/all_gather | solution.py:186
  203.9 233.8 %copy-start.223 = (f32[512]{0:T(512)}, f32[512]{0:T(512)S(1)}, u32[]{:S(2)}) copy-start(f32[512]{0:T(512)S(1)} %convert_element_type.104) | copy-start | bytes 6148
  279.6 37.7 %copy-start.235 = (bf16[64,128]{1,0:T(8,128)(2,1)S(1)}, bf16[64,128]{1,0:T(8,128)(2,1)}, u32[]{:S(2)}) copy-start(bf16[64,128]{1,0:T(8,128)(2,1)} %param.30) | copy-start | bytes 49156
  282.2 70.5 %all-to-all-start.2 = ((bf16[1024,4,128]{2,0,1:T(8,128)(2,1)}), bf16[1024,4,128]{2,0,1:T(8,128)(2,1)}, u32[]{:S(2)}, u32[]{:S(2)}) async-start(bf16[1024,4,128]{2,0,1:T(8,128)(2,1)} %copy_bitcast_fusion), calls=%async_computation.3 | async-start | bytes 2097152 | tf_op jit(solution)/shard_map/all_to_all | solution.py:199
  286.4 151.3 %reduce-scatter.20.cloned.1.call-start = ((), (), s32[]{:S(2)}) async-start(), calls=%async_computation.15 | async-start | bytes 10485760 | tf_op jit(solution)/shard_map/reduce_scatter | solution.py:216
  364.6 112.3 %all-gather.8.cloned.1.call-start = ((), (), s32[]{:S(2)}) async-start(), calls=%async_computation.16 | async-start | bytes 5242880 | tf_op jit(solution)/shard_map/all_gather | solution.py:225
  442.2 186.0 %reduce-scatter.22.cloned.1.call-start = ((), (), s32[]{:S(2)}) async-start(), calls=%async_computation.17 | async-start | bytes 5242880 | tf_op jit(solution)/shard_map/reduce_scatter | solution.py:245
  446.7 9.9 copy-start.40
  446.7 9.9 copy-start.42
  488.9 21.9 %copy-start.103 = (f32[256,64]{1,0:T(8,128)}, f32[256,64]{1,0:T(8,128)S(1)}, u32[]{:S(2)}) copy-start(f32[256,64]{1,0:T(8,128)S(1)} %get-tuple-element.248) | copy-start | bytes 196612
  500.8 28.1 %copy-start.206 = (f32[127,128]{1,0:T(8,128)S(1)}, f32[127,128]{1,0:T(8,128)}, u32[]{:S(2)}) copy-start(f32[127,128]{1,0:T(8,128)} %slice.1920) | copy-start | bytes 195076
  511.4 20.2 %copy-start.211 = (f32[127,128]{1,0:T(8,128)S(1)}, f32[127,128]{1,0:T(8,128)}, u32[]{:S(2)}) copy-start(f32[127,128]{1,0:T(8,128)} %slice.2051) | copy-start | bytes 195076
  547.4 9.2 copy-start.66
  578.1 115.6 %reduce-scatter.24.cloned.1.call-start = ((), (), s32[]{:S(2)}) async-start(), calls=%async_computation.18 | async-start | bytes 294912 | tf_op jit(solution)/shard_map/reduce_scatter | solution.py:277
  585.5 89.7 %all-to-all-start.1 = ((bf16[4,1024,128]{2,1,0:T(8,128)(2,1)}), bf16[4,1024,128]{2,1,0:T(8,128)(2,1)}, u32[]{:S(2)}, u32[]{:S(2)}) async-start(bf16[4,1024,128]{2,1,0:T(8,128)(2,1)} %bitcast.523), calls=%async_computation.2 | async-start | bytes 2097152 | tf_op jit(solution)/shard_map/all_to_all | solution.py:195
  589.9 168.4 %reduce-scatter.26.cloned.1.call-start = ((), (), s32[]{:S(2)}) async-start(), calls=%async_computation.19 | async-start | bytes 294912 | tf_op jit(solution)/shard_map/reduce_scatter | solution.py:278
  595.4 227.5 %reduce-scatter.34.cloned.1.call-start = ((), (), s32[]{:S(2)}) async-start(), calls=%async_computation.23 | async-start | bytes 294912
  600.1 287.3 %reduce-scatter.32.cloned.1.call-start = ((), (), s32[]{:S(2)}) async-start(), calls=%async_computation.22 | async-start | bytes 294912
  607.8 344.2 %reduce-scatter.30.cloned.1.call-start = ((), (), s32[]{:S(2)}) async-start(), calls=%async_computation.21 | async-start | bytes 294912
  613.6 402.8 %reduce-scatter.28.cloned.1.call-start = ((), (), s32[]{:S(2)}) async-start(), calls=%async_computation.20 | async-start | bytes 294912
  613.7 14.5 %copy-start.3 = (bf16[1024,512]{1,0:T(8,128)(2,1)S(1)}, bf16[1024,512]{1,0:T(8,128)(2,1)}, u32[]{:S(2)}) copy-start(bf16[1024,512]{1,0:T(8,128)(2,1)} %fusion.28) | copy-start | bytes 3145732
  613.7 14.5 %copy-start.214 = (f32[1024]{0:T(1024)S(1)}, f32[1024]{0:T(1024)}, u32[]{:S(2)}) copy-start(f32[1024]{0:T(1024)} %copy-done.212) | copy-start | bytes 12292
  613.7 14.5 %copy-start.217 = (f32[1024]{0:T(1024)S(1)}, f32[1024]{0:T(1024)}, u32[]{:S(2)}) copy-start(f32[1024]{0:T(1024)} %copy-done.215) | copy-start | bytes 12292
  613.7 14.5 %copy-start.221 = (f32[512]{0:T(512)S(1)}, f32[512]{0:T(512)}, u32[]{:S(2)}) copy-start(f32[512]{0:T(512)} %copy-done.219) | copy-start | bytes 6148
  613.7 14.5 %copy-start.224 = (f32[512]{0:T(512)S(1)}, f32[512]{0:T(512)}, u32[]{:S(2)}) copy-start(f32[512]{0:T(512)} %copy-done.223) | copy-start | bytes 6148
  613.7 14.5 %copy-start.227 = (f32[512]{0:T(512)S(1)}, f32[512]{0:T(512)}, u32[]{:S(2)}) copy-start(f32[512]{0:T(512)} %copy-done.225) | copy-start | bytes 6148
  616.6 14.5 %copy-start.242 = (f32[512]{0:T(512)S(1)}, f32[512]{0:T(512)}, u32[]{:S(2)}) copy-start(f32[512]{0:T(512)} %copy-done.241) | copy-start | bytes 6148
  616.6 14.5 %copy-start.244 = (f32[512]{0:T(512)S(1)}, f32[512]{0:T(512)}, u32[]{:S(2)}) copy-start(f32[512]{0:T(512)} %copy-done.243) | copy-start | bytes 6148
  616.7 58.5 %copy-start.8 = (bf16[1024,512]{1,0:T(8,128)(2,1)S(1)}, bf16[1024,512]{1,0:T(8,128)(2,1)}, u32[]{:S(2)}) copy-start(bf16[1024,512]{1,0:T(8,128)(2,1)} %param.33) | copy-start | bytes 3145732
  616.7 58.5 %copy-start.229 = (f32[1024]{0:T(1024)S(1)}, f32[1024]{0:T(1024)}, u32[]{:S(2)}) copy-start(f32[1024]{0:T(1024)} %copy-done.228) | copy-start | bytes 12292
  (226 other events, 579.3 us)
Sparse Core Ops, SparseCore 0:
  46.0 31.7 all-gather.3
  203.4 72.5 reduce-scatter.17
  279.6 45.2 all-gather.5
  364.7 72.9 reduce-scatter.19
  442.3 34.4 all-gather.7
  578.2 49.9 reduce-scatter.21
  632.5 61.2 reduce-scatter.23
  698.0 60.3 reduce-scatter.25
  762.6 60.2 reduce-scatter.33
  827.0 60.2 reduce-scatter.31
  891.6 60.2 reduce-scatter.29
  956.0 60.2 reduce-scatter.27
